TPU v7x, 512 devices: a whole 4x4x16 slice. The times are simulated.
512 devices in a mesh: dp: 16 (over x, y), heads: 16 (over z), side: 2 (over core).
Axes of the slice: x: 4, y: 4, z: 16, core: 2. Of those that a mesh axis runs over, the one named last changes fastest.
Arguments:
- queries: bfloat16 [384, 2, 4096], P('dp', None, ('heads', 'side')), may hold values from -6 to 6
- new_keys: bfloat16 [384, 2, 4096], P('dp', None, ('heads', 'side')), may hold values from -6 to 6
- new_values: bfloat16 [384, 2, 4096], P('dp', None, ('heads', 'side')), may hold values from -6 to 6
- head_states: bfloat16 [384, 32, 128, 128], P('dp', ('heads', 'side')), may hold values from -6 to 6
- slopes: float32 [32], P(('heads', 'side')), may hold values from 0.004 to 0.9
- head_gain: float32 [4096], P(('heads', 'side')), may hold values from 0.5 to 1.5
- out_weight: bfloat16 [4096, 3072], P(('heads', 'side')), may hold values from -0.1875 to 0.1875
- residual: bfloat16 [384, 2, 3072], P('dp', None, ('heads', 'side')), may hold values from -10 to 10
- norm_gain: float32 [3072], replicated, may hold values from 0.5 to 1.5
- expert_ids: int32 [384, 2, 2], P('dp'), may hold values from 0 to 15, all different within a row; in each aligned block of 48 rows (0 to 47, 48 to 95, ..., all dimensions but the last counted through in order) at most 9 rows name the same one
- expert_gates: float32 [384, 2, 2], P('dp'), may hold values from 0.2 to 1
- w_gate: bfloat16 [16, 16, 192, 4608], P('dp', None, 'side', 'heads'), may hold values from -0.109375 to 0.109375
- w_up: bfloat16 [16, 16, 192, 4608], P('dp', None, 'side', 'heads'), may hold values from -0.109375 to 0.109375
- w_down: bfloat16 [16, 4608, 16, 192], P('dp', 'heads', None, 'side'), may hold values from -0.125 to 0.125
Outputs:
- state_out: bfloat16 [384, 32, 128, 128], P('dp', ('heads', 'side'))
- resid_out: bfloat16 [384, 2, 3072], P('dp', None, ('heads', 'side'))
- moe_out: bfloat16 [384, 2, 3072], P('dp', None, ('heads', 'side'))
Inputs may be any that keep to these rules, and one draw needn't show every extreme that they name: `expert_ids`: among the 48 tokens of one dp index a token's 2 experts differ, no expert is chosen by more than 9 of them, and some expert is chosen by exactly 9.
All inputs are finite; a program needn't handle non-finite values.
Results may differ from a plain program's by a relative error of at most 0.025.
Values may be sent and summed in bfloat16 or wider, within the bound.
A program may use at most 64 MiB of HBM per device.

v0:
```python
import jax
import jax.numpy as jnp
from jax import lax
from jax.sharding import PartitionSpec as P


def local(
    queries,
    new_keys,
    new_values,
    head_states,
    slopes,
    head_gain,
    out_weight,
    residual,
    norm_gain,
    expert_ids,
    expert_gates,
    w_gate,
    w_up,
    w_down,
):
    requests_dev, step_count, inner_width = queries.shape
    local_heads = slopes.shape[0]
    head_size = inner_width // local_heads
    query_rows = queries.astype(jnp.float32).reshape(
        requests_dev, step_count, local_heads, head_size
    )
    key_rows = new_keys.astype(jnp.float32).reshape(
        requests_dev, step_count, local_heads, head_size
    )
    value_rows = new_values.astype(jnp.float32).reshape(
        requests_dev, step_count, local_heads, head_size
    )
    decays = jnp.exp(-slopes)[None, :, None, None]
    current = head_states.astype(jnp.float32)
    outputs = []
    for step in range(step_count):
        current = decays * current + key_rows[:, step, :, :, None] * value_rows[:, step, :, None, :]
        outputs.append(
            jnp.einsum(
                "rhi,rhij->rhj", query_rows[:, step], current, precision=lax.Precision.HIGHEST
            )
        )
    state_out = current.astype(jnp.bfloat16)
    head_output = jnp.stack(outputs, 1)
    scaled = head_output * lax.rsqrt(jnp.mean(head_output * head_output, -1, keepdims=True) + 1e-06)
    tokens_dev = requests_dev * step_count
    normed = (
        (scaled * head_gain.reshape(local_heads, head_size))
        .astype(jnp.bfloat16)
        .reshape(tokens_dev, inner_width)
    )
    partial_out = jnp.dot(normed, out_weight, preferred_element_type=jnp.float32)
    attention = lax.psum_scatter(partial_out, ("heads", "side"), scatter_dimension=1, tiled=True)
    width = norm_gain.shape[0]
    piece_width = attention.shape[1]
    resid_new = (residual.reshape(tokens_dev, piece_width).astype(jnp.float32) + attention).astype(
        jnp.bfloat16
    )
    stream = resid_new.astype(jnp.float32)
    sum_squares = lax.psum(jnp.sum(stream * stream, 1), ("heads", "side"))
    gain_piece = lax.dynamic_slice_in_dim(
        norm_gain, lax.axis_index(("heads", "side")) * piece_width, piece_width
    )
    mixed_in = (stream * lax.rsqrt(sum_squares / width + 1e-06)[:, None] * gain_piece).astype(
        jnp.bfloat16
    )
    groups = lax.axis_size("dp")
    heads_count = lax.axis_size("heads")
    choices_each = expert_ids.shape[2]
    capacity = max(2, 3 * choices_each * tokens_dev // (2 * groups))
    flat_ids = expert_ids.reshape(-1)
    onehot_table = (flat_ids[:, None] == jnp.arange(groups, dtype=jnp.int32)[None, :]).astype(
        jnp.int32
    )
    earlier = jnp.cumsum(onehot_table, 0) - onehot_table
    slot_index = jnp.sum(earlier * onehot_table, 1)
    target = flat_ids * capacity + slot_index
    source_row = jnp.arange(tokens_dev * choices_each, dtype=jnp.int32) // choices_each
    gate_flat = w_gate[0].reshape(-1, w_gate.shape[3])
    up_flat = w_up[0].reshape(-1, w_up.shape[3])
    down_flat = w_down[0].reshape(w_down.shape[1], -1)
    holder = jnp.zeros((groups * capacity, mixed_in.shape[1]), mixed_in.dtype)
    arrived = lax.all_to_all(
        holder.at[target].set(mixed_in[source_row]).reshape(groups, capacity, mixed_in.shape[1]),
        "dp",
        split_axis=0,
        concat_axis=0,
        tiled=True,
    )
    piece = lax.all_gather(arrived, "heads", axis=2, tiled=True)
    flat_piece = piece.reshape(-1, piece.shape[2])
    gate_part = jnp.dot(flat_piece, gate_flat, preferred_element_type=jnp.float32)
    up_part = jnp.dot(flat_piece, up_flat, preferred_element_type=jnp.float32)
    gate_val, up_val = (
        lax.psum(gate_part.astype(jnp.bfloat16), "side").astype(jnp.float32),
        lax.psum(up_part.astype(jnp.bfloat16), "side").astype(jnp.float32),
    )
    activation = (jax.nn.silu(gate_val) * up_val).astype(jnp.bfloat16)
    down_part = jnp.dot(activation, down_flat, preferred_element_type=jnp.float32).reshape(
        groups, capacity, heads_count, piece_width
    )
    reduced = lax.psum_scatter(
        down_part.astype(jnp.bfloat16), "heads", scatter_dimension=2, tiled=True
    )
    returned = lax.all_to_all(reduced, "dp", split_axis=0, concat_axis=0, tiled=True)
    picked = returned.reshape(groups * capacity, piece_width)[target].astype(jnp.float32)
    weighted = picked * expert_gates.reshape(-1)[:, None]
    moe_out = jnp.sum(weighted.reshape(tokens_dev, choices_each, piece_width), 1).astype(
        jnp.bfloat16
    )
    return (
        state_out,
        resid_new.reshape(requests_dev, step_count, piece_width),
        moe_out.reshape(requests_dev, step_count, piece_width),
    )


def solution(mesh):
    return jax.shard_map(
        local,
        mesh=mesh,
        in_specs=(
            P("dp", None, ("heads", "side")),
            P("dp", None, ("heads", "side")),
            P("dp", None, ("heads", "side")),
            P("dp", ("heads", "side"), None, None),
            P(("heads", "side")),
            P(("heads", "side")),
            P(("heads", "side"), None),
            P("dp", None, ("heads", "side")),
            P(),
            P("dp", None, None),
            P("dp", None, None),
            P("dp", None, "side", "heads"),
            P("dp", None, "side", "heads"),
            P("dp", "heads", None, "side"),
        ),
        out_specs=(
            P("dp", ("heads", "side"), None, None),
            P("dp", None, ("heads", "side")),
            P("dp", None, ("heads", "side")),
        ),
        check_vma=False,
    )
```

profile of v0, /device:TPU:32, one launch (start us, length us, event | category | flops | bytes accessed | tf_op | source)
XLA Modules:
  0.0 491.2 jit_solution(13953203980056573112)
XLA Ops:
  7.2 0.8 bitcast_convert_fusion.1
  8.1 0.7 bitcast_convert_fusion
  9.6 0.7 copy.73
  10.3 2.2 fusion.5
  12.5 1.8 fusion.8
  14.3 0.1 multiply_reduce_fusion
  14.4 0.1 rsqrt.15
  14.6 1.6 convolution_bitcast_fusion
  16.3 0.1 copy.43
  16.4 0.1 eq.15
  16.5 0.1 fusion.26
  16.6 0.1 reduce_window_sum.11
  16.7 0.1 copy.42
  16.8 0.1 mul.182
  17.0 0.8 dynamic_slice.3
  17.8 0.2 select_reduce_fusion
  17.9 110.4 %reduce-scatter.7.cloned.1.call-done = f32[96,48]{1,0:T(8,128)} async-done(((f32[3072,48]{1,0:T(8,128)}), f32[96,48]{1,0:T(8,128)}) %reduce-scatter.7.cloned.1.call-update) | async-done | bytes 18448
  128.3 0.9 copy.61
  129.2 0.1 fusion.27
  129.3 46.0 %psum.21 = f32[48]{0:T(128)S(1)} all-reduce(f32[48]{0:T(128)S(1)} %get-tuple-element.5), channel_id=1, replica_groups=mesh['dp'=16,'heads'=16,'side'=2] {'heads','side'}, use_global_device_ids=true, to_apply=%region_5.6 | all-reduce | flops 48 | bytes 384 | tf_op jit(solution)/shard_map/psum | solution.py:62
  175.3 0.1 fusion.29
  175.4 1.0 scatter_custom_fusion
  176.5 0.1 reshape.300
  176.6 14.1 %all_to_all.10 = bf16[16,2,432]{2,1,0:T(2,128)(2,1)S(1)} all-to-all(bf16[16,2,432]{2,1,0:T(2,128)(2,1)S(1)} %reshape.300), channel_id=1, replica_groups=mesh['dp'=16,'heads'=16,'side'=2] {'dp'}, dimensions={0} | all-to-all | bytes 55296 | tf_op jit(solution)/shard_map/all_to_all | solution.py:85
  190.7 0.1 reshape.301
  190.8 0.4 copy.44
  191.2 83.1 %all_gather.3 = bf16[16,9,1536]{1,0,2:T(8,128)(2,1)} all-gather(bf16[16,9,96]{1,0,2:T(8,128)(2,1)S(1)} %copy.44), channel_id=1, replica_groups=mesh['dp'=16,'heads'=16,'side'=2] {'heads'}, dimensions={2}, use_global_device_ids=true | all-gather | bytes 470016 | tf_op jit(solution)/shard_map/all_gather | solution.py:92
  274.3 8.2 %reshape.288 = bf16[144,1536]{0,1:T(8,128)(2,1)S(1)} reshape(bf16[16,9,1536]{1,0,2:T(8,128)(2,1)} %all_gather.3) | data formatting | bytes 884736 | tf_op jit(solution)/shard_map/reshape | solution.py:93
  282.5 1.1 convolution_convert_fusion.1
  283.6 0.2 copy-done.1
  283.8 1.1 convolution_convert_fusion.2
  285.0 2.4 reshape_squeeze.11
  287.3 0.7 copy.46
  288.1 36.6 %all-reduce.7.cloned.1.call-done = (bf16[144,288]{1,0:T(8,128)(2,1)}, bf16[144,288]{1,0:T(8,128)(2,1)}) async-done(((bf16[144,288]{1,0:T(8,128)(2,1)}, bf16[144,288]{1,0:T(8,128)(2,1)}), (bf16[144,288]{1,0:T(8,128)(2,1)}, bf16[144,288]{1,0:T(8,128)(2,1)})) %all-reduce.7.cloned.1.call-update) | async-done | bytes 165904 | tf_op jit(solution)/shard_map/psum | solution.py:98
  324.7 1.0 fusion.23
  325.7 0.1 dot_general.29
  325.8 1.6 convolution_convert_fusion
  327.4 1.3 dynamic-slice
  328.7 1.7 fusion.4
  330.5 136.0 %all-reduce.5.cloned.1.call-done = bf16[16,9,16,96]{3,0,2,1:T(8,128)(2,1)} async-done(((bf16[16,9,16,96]{3,0,2,1:T(8,128)(2,1)}), bf16[16,9,16,96]{3,0,2,1:T(8,128)(2,1)}) %all-reduce.5.cloned.1.call-update) | async-done | bytes 442384
  466.5 1.4 constant_dynamic-slice_fusion
  467.9 0.7 reshape.302
  468.6 6.8 %all-to-all-start.1 = ((bf16[16,2,432]{2,1,0:T(2,128)(2,1)}), bf16[16,2,432]{2,1,0:T(2,128)(2,1)S(1)}, u32[]{:S(2)}, u32[]{:S(2)}) async-start(bf16[16,2,432]{2,1,0:T(2,128)(2,1)} %reshape.302), calls=%async_computation.1 | async-start | bytes 65536 | tf_op jit(solution)/shard_map/all_to_all | solution.py:107
  475.5 0.1 copy.59
  475.6 7.5 %all-to-all-done.1 = bf16[16,2,432]{2,1,0:T(2,128)(2,1)S(1)} async-done(((bf16[16,2,432]{2,1,0:T(2,128)(2,1)}), bf16[16,2,432]{2,1,0:T(2,128)(2,1)S(1)}, u32[]{:S(2)}, u32[]{:S(2)}) %all-to-all-start.1) | async-done | bytes 27680 | tf_op jit(solution)/shard_map/all_to_all | solution.py:107
  483.1 0.1 reshape.303
  483.2 0.7 gather_fusion
  483.9 0.7 fusion.25
  (38 shorter events, 0.4 us)
Async XLA Ops:
  7.2 275.4 %copy-start = (bf16[1,16,96,288]{3,2,1,0:T(8,128)(2,1)S(1)}, bf16[1,16,96,288]{3,2,1,0:T(8,128)(2,1)}, u32[]{:S(2)}) copy-start(bf16[1,16,96,288]{3,2,1,0:T(8,128)(2,1)} %param.26) | copy-start | bytes 2654212
  7.2 5.3 %copy-start.2 = (bf16[24,1,128,128]{3,2,1,0:T(8,128)(2,1)S(1)}, bf16[24,1,128,128]{3,2,1,0:T(8,128)(2,1)}, u32[]{:S(2)}) copy-start(bf16[24,1,128,128]{3,2,1,0:T(8,128)(2,1)} %param.17) | copy-start | bytes 2359300
  7.2 121.1 %reduce-scatter.7.cloned.1.call-start = ((), (), s32[]{:S(2)}) async-start(), calls=%async_computation.3 | async-start | bytes 1622016
  12.5 2.0 copy-start.4
  12.5 2.1 copy-start.9
  14.5 1.7 copy-start.7
  16.2 113.0 %copy-start.6 = (bf16[24,2,96]{2,1,0:T(2,128)(2,1)S(1)}, bf16[24,2,96]{2,1,0:T(2,128)(2,1)}, u32[]{:S(2)}) copy-start(bf16[24,2,96]{2,1,0:T(2,128)(2,1)} %param.21) | copy-start | bytes 27652
  16.2 308.5 %all-reduce.7.cloned.1.call-start = ((), (), s32[]{:S(2)}) async-start(), calls=%async_computation.5 | async-start | bytes 442368 | tf_op jit(solution)/shard_map/psum | solution.py:98
  129.3 145.0 %copy-start.5 = (bf16[48,96]{1,0:T(8,128)(2,1)}, bf16[48,96]{1,0:T(8,128)(2,1)S(1)}, u32[]{:S(2)}) copy-start(bf16[48,96]{1,0:T(8,128)(2,1)S(1)} %get-tuple-element.6) | copy-start | bytes 27652
  282.5 1.3 copy-start.1
  284.9 181.6 %all-reduce.5.cloned.1.call-start = ((), (), s32[]{:S(2)}) async-start(), calls=%async_computation.4 | async-start | bytes 1179648
  288.0 40.7 %copy-start.3 = (bf16[24,1,128,128]{3,2,1,0:T(8,128)(2,1)S(1)}, bf16[24,1,128,128]{3,2,1,0:T(8,128)(2,1)}, u32[]{:S(2)}) copy-start(bf16[24,1,128,128]{3,2,1,0:T(8,128)(2,1)} %param.17) | copy-start | bytes 2359300
  327.4 148.1 %copy-start.8 = (f32[24,2,2]{0,2,1:T(2,128)S(1)}, f32[24,2,2]{0,2,1:T(2,128)}, u32[]{:S(2)}) copy-start(f32[24,2,2]{0,2,1:T(2,128)} %param.24) | copy-start | bytes 1156
  468.6 14.4 %all-to-all-start.1 = ((bf16[16,2,432]{2,1,0:T(2,128)(2,1)}), bf16[16,2,432]{2,1,0:T(2,128)(2,1)S(1)}, u32[]{:S(2)}, u32[]{:S(2)}) async-start(bf16[16,2,432]{2,1,0:T(2,128)(2,1)} %reshape.302), calls=%async_computation.1 | async-start | bytes 65536 | tf_op jit(solution)/shard_map/all_to_all | solution.py:107
Sparse Core Ops, SparseCore 0:
  16.3 111.9 reduce-scatter.6
  285.0 39.6 all-reduce.6
  327.5 138.9 all-reduce.4
where the time goes:
time: 492 us; the launch traced here: 491 us
  waiting for transfers between devices  291 us (59%)
  blocking collectives  143 us (29%)
  local copies, waits for them, and re-layouts  20.6 us (4%)
  between operations  14.7 us (3%)
  matrix products  9.36 us (2%)
  starting transfers between devices  6.93 us (1%)
  other arithmetic  5.83 us (1%)
    unnamed x5, waiting for transfers between devices  246 us
    all_gather x1, blocking collectives, local(): piece = lax.all_gather(arrived, 'heads', axis=2, tiled=True)  83.1 us
    psum x1, blocking collectives, local(): sum_squares = lax.psum(jnp.sum(stream * stream, 1), ('heads', 'side'))  46 us
    psum x1, waiting for transfers between devices, local(): lax.psum(up_part.astype(jnp.bfloat16), 'side').astype(jnp.float32)  36.6 us
    all_to_all x1, blocking collectives, local(): lax.all_to_all(holder.at[target].set(mixed_in[source_row]).reshape(groups...  14.1 us
  transfers between devices with their start and end apart: 4, of which 4 were waited for; matrix products, arithmetic and copies ran while one was open for 2% of the time, Pallas kernels for 0%

commit v1 on v0

--- a/solution.py
+++ b/solution.py
@@ -59,7 +59,7 @@
         jnp.bfloat16
     )
     stream = resid_new.astype(jnp.float32)
-    sum_squares = lax.psum(jnp.sum(stream * stream, 1), ("heads", "side"))
+    sum_squares = lax.psum(lax.psum(jnp.sum(stream * stream, 1), "side"), "heads")
     gain_piece = lax.dynamic_slice_in_dim(
         norm_gain, lax.axis_index(("heads", "side")) * piece_width, piece_width
     )

time: 492 us -> 469 us (0.953)
  blocking collectives: 143 us -> 123 us
    psum x1 -> x2, blocking collectives: 46 us -> 33.2 us  [the longest x1 30.7 us: local(): lax.psum(lax.psum(jnp.sum(stream * stream, 1), 'side'), 'heads')]
    all_gather x1, blocking collectives: 83.1 us -> 75.2 us  [local(): piece = lax.all_gather(arrived, 'heads', axis=2, tiled=True)]
where the time goes in v1:
time: 469 us; the launch traced here: 468 us
  waiting for transfers between devices  288 us (61%)
  blocking collectives  123 us (26%)
  local copies, waits for them, and re-layouts  20.6 us (4%)
  between operations  14.7 us (3%)
  matrix products  9.36 us (2%)
  starting transfers between devices  6.93 us (1%)
  other arithmetic  5.83 us (1%)
    unnamed x5, waiting for transfers between devices  246 us
    all_gather x1, blocking collectives, local(): piece = lax.all_gather(arrived, 'heads', axis=2, tiled=True)  75.2 us
    psum x1, waiting for transfers between devices, local(): lax.psum(up_part.astype(jnp.bfloat16), 'side').astype(jnp.float32)  34.3 us
    psum x1, blocking collectives, local(): lax.psum(lax.psum(jnp.sum(stream * stream, 1), 'side'), 'heads')  30.7 us
    all_to_all x1, blocking collectives, local(): lax.all_to_all(holder.at[target].set(mixed_in[source_row]).reshape(groups...  14.2 us
  transfers between devices with their start and end apart: 4, of which 4 were waited for; matrix products, arithmetic and copies ran while one was open for 2% of the time, Pallas kernels for 0%

profile of v1, /device:TPU:32, one launch (start us, length us, event | category | flops | bytes accessed | tf_op | source)
XLA Modules:
  0.0 468.3 jit_solution(3205356275488727703)
XLA Ops:
  7.2 0.8 bitcast_convert_fusion.1
  8.1 0.7 bitcast_convert_fusion
  9.6 0.7 copy.73
  10.3 2.2 fusion.5
  12.5 1.8 fusion.8
  14.3 0.1 multiply_reduce_fusion
  14.4 0.1 rsqrt.15
  14.6 1.6 convolution_bitcast_fusion
  16.3 0.1 copy.43
  16.4 0.1 eq.15
  16.5 0.1 fusion.26
  16.6 0.1 reduce_window_sum.11
  16.7 0.1 copy.42
  16.8 0.1 mul.182
  17.0 0.8 dynamic_slice.3
  17.8 0.2 select_reduce_fusion
  17.9 110.4 %reduce-scatter.7.cloned.1.call-done = f32[96,48]{1,0:T(8,128)} async-done(((f32[3072,48]{1,0:T(8,128)}), f32[96,48]{1,0:T(8,128)}) %reduce-scatter.7.cloned.1.call-update) | async-done | bytes 18448
  128.3 0.9 copy.61
  129.2 0.1 fusion.27
  129.3 2.5 psum.28
  131.8 30.7 %psum.29 = f32[48]{0:T(128)S(1)} all-reduce(f32[48]{0:T(128)S(1)} %psum.28), channel_id=1, replica_groups=mesh['dp'=16,'heads'=16,'side'=2] {'heads'}, use_global_device_ids=true, to_apply=%region_6.7 | all-reduce | flops 48 | bytes 384 | tf_op jit(solution)/shard_map/psum | solution.py:62
  162.5 0.1 fusion.29
  162.6 1.0 scatter_custom_fusion
  163.7 0.1 reshape.300
  163.8 14.2 %all_to_all.10 = bf16[16,2,432]{2,1,0:T(2,128)(2,1)S(1)} all-to-all(bf16[16,2,432]{2,1,0:T(2,128)(2,1)S(1)} %reshape.300), channel_id=1, replica_groups=mesh['dp'=16,'heads'=16,'side'=2] {'dp'}, dimensions={0} | all-to-all | bytes 55296 | tf_op jit(solution)/shard_map/all_to_all | solution.py:85
  178.0 0.1 reshape.301
  178.2 0.4 copy.44
  178.5 75.2 %all_gather.3 = bf16[16,9,1536]{1,0,2:T(8,128)(2,1)} all-gather(bf16[16,9,96]{1,0,2:T(8,128)(2,1)S(1)} %copy.44), channel_id=1, replica_groups=mesh['dp'=16,'heads'=16,'side'=2] {'heads'}, dimensions={2}, use_global_device_ids=true | all-gather | bytes 470016 | tf_op jit(solution)/shard_map/all_gather | solution.py:92
  253.8 8.2 %reshape.288 = bf16[144,1536]{0,1:T(8,128)(2,1)S(1)} reshape(bf16[16,9,1536]{1,0,2:T(8,128)(2,1)} %all_gather.3) | data formatting | bytes 884736 | tf_op jit(solution)/shard_map/reshape | solution.py:93
  262.0 1.1 convolution_convert_fusion.1
  263.1 0.2 copy-done.1
  263.3 1.1 convolution_convert_fusion.2
  264.5 2.4 reshape_squeeze.11
  266.8 0.7 copy.46
  267.5 34.3 %all-reduce.7.cloned.1.call-done = (bf16[144,288]{1,0:T(8,128)(2,1)}, bf16[144,288]{1,0:T(8,128)(2,1)}) async-done(((bf16[144,288]{1,0:T(8,128)(2,1)}, bf16[144,288]{1,0:T(8,128)(2,1)}), (bf16[144,288]{1,0:T(8,128)(2,1)}, bf16[144,288]{1,0:T(8,128)(2,1)})) %all-reduce.7.cloned.1.call-update) | async-done | bytes 165904 | tf_op jit(solution)/shard_map/psum | solution.py:98
  301.8 1.0 fusion.23
  302.9 1.6 convolution_convert_fusion
  304.5 1.3 dynamic-slice
  305.9 1.7 fusion.4
  307.6 136.0 %all-reduce.5.cloned.1.call-done = bf16[16,9,16,96]{3,0,2,1:T(8,128)(2,1)} async-done(((bf16[16,9,16,96]{3,0,2,1:T(8,128)(2,1)}), bf16[16,9,16,96]{3,0,2,1:T(8,128)(2,1)}) %all-reduce.5.cloned.1.call-update) | async-done | bytes 442384
  443.6 1.4 constant_dynamic-slice_fusion
  445.0 0.7 reshape.302
  445.7 6.8 %all-to-all-start.1 = ((bf16[16,2,432]{2,1,0:T(2,128)(2,1)}), bf16[16,2,432]{2,1,0:T(2,128)(2,1)S(1)}, u32[]{:S(2)}, u32[]{:S(2)}) async-start(bf16[16,2,432]{2,1,0:T(2,128)(2,1)} %reshape.302), calls=%async_computation.1 | async-start | bytes 65536 | tf_op jit(solution)/shard_map/all_to_all | solution.py:107
  452.6 0.1 copy.59
  452.7 7.5 %all-to-all-done.1 = bf16[16,2,432]{2,1,0:T(2,128)(2,1)S(1)} async-done(((bf16[16,2,432]{2,1,0:T(2,128)(2,1)}), bf16[16,2,432]{2,1,0:T(2,128)(2,1)S(1)}, u32[]{:S(2)}, u32[]{:S(2)}) %all-to-all-start.1) | async-done | bytes 27680 | tf_op jit(solution)/shard_map/all_to_all | solution.py:107
  460.1 0.1 reshape.303
  460.3 0.7 gather_fusion
  461.0 0.7 fusion.25
  (39 shorter events, 0.4 us)
Async XLA Ops:
  7.2 254.8 %copy-start = (bf16[1,16,96,288]{3,2,1,0:T(8,128)(2,1)S(1)}, bf16[1,16,96,288]{3,2,1,0:T(8,128)(2,1)}, u32[]{:S(2)}) copy-start(bf16[1,16,96,288]{3,2,1,0:T(8,128)(2,1)} %param.26) | copy-start | bytes 2654212
  7.2 5.3 %copy-start.2 = (bf16[24,1,128,128]{3,2,1,0:T(8,128)(2,1)S(1)}, bf16[24,1,128,128]{3,2,1,0:T(8,128)(2,1)}, u32[]{:S(2)}) copy-start(bf16[24,1,128,128]{3,2,1,0:T(8,128)(2,1)} %param.17) | copy-start | bytes 2359300
  7.2 121.1 %reduce-scatter.7.cloned.1.call-start = ((), (), s32[]{:S(2)}) async-start(), calls=%async_computation.3 | async-start | bytes 1622016
  12.5 2.0 copy-start.4
  12.5 2.1 copy-start.9
  14.5 1.7 copy-start.7
  16.2 113.0 %copy-start.6 = (bf16[24,2,96]{2,1,0:T(2,128)(2,1)S(1)}, bf16[24,2,96]{2,1,0:T(2,128)(2,1)}, u32[]{:S(2)}) copy-start(bf16[24,2,96]{2,1,0:T(2,128)(2,1)} %param.21) | copy-start | bytes 27652
  16.2 285.6 %all-reduce.7.cloned.1.call-start = ((), (), s32[]{:S(2)}) async-start(), calls=%async_computation.5 | async-start | bytes 442368 | tf_op jit(solution)/shard_map/psum | solution.py:98
  129.3 124.4 %copy-start.5 = (bf16[48,96]{1,0:T(8,128)(2,1)}, bf16[48,96]{1,0:T(8,128)(2,1)S(1)}, u32[]{:S(2)}) copy-start(bf16[48,96]{1,0:T(8,128)(2,1)S(1)} %get-tuple-element.6) | copy-start | bytes 27652
  262.0 1.3 copy-start.1
  264.4 179.2 %all-reduce.5.cloned.1.call-start = ((), (), s32[]{:S(2)}) async-start(), calls=%async_computation.4 | async-start | bytes 1179648
  267.5 38.3 %copy-start.3 = (bf16[24,1,128,128]{3,2,1,0:T(8,128)(2,1)S(1)}, bf16[24,1,128,128]{3,2,1,0:T(8,128)(2,1)}, u32[]{:S(2)}) copy-start(bf16[24,1,128,128]{3,2,1,0:T(8,128)(2,1)} %param.17) | copy-start | bytes 2359300
  304.5 148.0 %copy-start.8 = (f32[24,2,2]{0,2,1:T(2,128)S(1)}, f32[24,2,2]{0,2,1:T(2,128)}, u32[]{:S(2)}) copy-start(f32[24,2,2]{0,2,1:T(2,128)} %param.24) | copy-start | bytes 1156
  445.7 14.4 %all-to-all-start.1 = ((bf16[16,2,432]{2,1,0:T(2,128)(2,1)}), bf16[16,2,432]{2,1,0:T(2,128)(2,1)S(1)}, u32[]{:S(2)}, u32[]{:S(2)}) async-start(bf16[16,2,432]{2,1,0:T(2,128)(2,1)} %reshape.302), calls=%async_computation.1 | async-start | bytes 65536 | tf_op jit(solution)/shard_map/all_to_all | solution.py:107
Sparse Core Ops, SparseCore 0:
  16.3 111.9 reduce-scatter.6
  264.5 37.2 all-reduce.6
  304.6 138.8 all-reduce.4
